TPU v7x, 32 devices: a whole 2x2x4 slice. The times are simulated.
32 devices in a mesh: gy: 8 (over y, x, core), gz: 4 (over z).
Axes of the slice: x: 2, y: 2, z: 4, core: 2. Of those that a mesh axis runs over, the one named last changes fastest.
Arguments:
- state: float32 [8, 5, 256, 512], P(None, None, 'gy', 'gz'), may hold values from -6 to 6
- conduct: float32 [8, 256, 512], P(None, 'gy', 'gz'), may hold values from 0.3 to 3
- y_bands: float32 [8, 5, 256, 512], P(None, None, 'gy', 'gz'), may hold values from -250 to 541, as said below
- z_bands: float32 [8, 5, 256, 512], P(None, None, 'gy', 'gz'), may hold values from -250 to 541, as said below
Outputs:
- new_state: float32 [8, 5, 256, 512], P(None, None, 'gy', 'gz')
Inputs may be any that keep to these rules, and one draw needn't show every extreme that they name: `y_bands`: in every cell band 2 exceeds the sum of the magnitudes of bands 0, 1, 3 and 4 by 0.03 or more; bands 1 and 3 are negative, bands 0 and 4 are not positive. `z_bands`: in every cell band 2 exceeds the sum of the magnitudes of bands 0, 1, 3 and 4 by 0.03 or more; bands 1 and 3 are negative, bands 0 and 4 are not positive.
All inputs are finite; a program needn't handle non-finite values.
Results may differ from a plain program's by a relative error of at most 0.0003.
Values sent between devices are 32-bit elements; how exact they have to be, the bound alone decides.
A program may use at most 192 MiB of HBM per device.

v0:
```python
import functools
import jax
import jax.numpy as jnp
from jax import lax
from jax.experimental import pallas as pl
from jax.experimental.pallas import tpu as pltpu
from jax.sharding import PartitionSpec as P

flux_tenth = 0.1
UNROLL = 32
MESH = pl.DeviceIdType.MESH
ROWS = 32
PACK = 20
STEP = ROWS + 1
HALF = ROWS // 2


def rows_loop(count, body, carry, unroll=UNROLL):
    if unroll >= count:
        for place in range(count):
            carry = body(place, carry)
        return carry

    def group(number, state):
        for inner in range(unroll):
            state = body(number * unroll + inner, state)
        return state

    return lax.fori_loop(0, count // unroll, group, carry)


def mm(a, b):
    return (
        a[0] * b[0] + a[1] * b[2],
        a[0] * b[1] + a[1] * b[3],
        a[2] * b[0] + a[3] * b[2],
        a[2] * b[1] + a[3] * b[3],
    )


def mv(a, x):
    return (a[0] * x[0] + a[1] * x[1], a[2] * x[0] + a[3] * x[1])


def plus(a, b):
    return tuple(x + y for x, y in zip(a, b))


def minus(a, b):
    return tuple(x - y for x, y in zip(a, b))


def negative(a):
    return tuple(-x for x in a)


def one_minus_inverse(k):
    m00, m01, m10, m11 = 1.0 - k[0], -k[1], -k[2], 1.0 - k[3]
    scale = 1.0 / (m00 * m11 - m01 * m10)
    return (m11 * scale, -m01 * scale, -m10 * scale, m00 * scale)


def factor_segment(band, coefs, spikes):
    zero = jnp.zeros((8, 128), jnp.float32)

    def one_row(j, carry, left):
        p1, q1, p2, q2, l01, l11, l02, l12 = carry
        a, b, c, d, e = (band(k, j) for k in range(5))
        red = b - a * p2
        inv = 1.0 / (c - a * q2 - red * p1)
        p = (d - red * q1) * inv
        q = e * inv
        ai = a * inv
        ri = red * inv
        if left == 0:
            l0, l1 = ai, b * inv
        elif left == 1:
            l0, l1 = -ri * l01, ai - ri * l11
        else:
            l0 = -ai * l02 - ri * l01
            l1 = -ai * l12 - ri * l11
        for number, item in enumerate((ai, ri, inv, p, q)):
            coefs[j, number] = item
        spikes[j, 0] = l0
        spikes[j, 1] = l1
        return (p, q, p1, q1, l0, l1, l01, l11)

    carry = (zero,) * 8
    carry = one_row(0, carry, 0)
    carry = one_row(1, carry, 1)
    carry = rows_loop(ROWS - 2, lambda j, c: one_row(j + 2, c, 2), carry, 30)

    def back(i, carry):
        j = ROWS - 1 - i
        one, two = carry
        p, q = coefs[j, 3], coefs[j, 4]
        start = (spikes[j, 0], spikes[j, 1], zero, zero)
        new = tuple(s - p * x - q * y for s, x, y in zip(start, one, two))
        for number in range(4):
            spikes[j, number] = new[number]
        return (new, one)

    minus_one = zero - 1.0
    rows_loop(ROWS, back, ((zero, zero, minus_one, zero), (zero, zero, zero, minus_one)))


def forward_values(rhs, coefs, values):
    zero = jnp.zeros((8, 128), jnp.float32)

    def row(j, carry):
        one, two = carry
        ai, ri, inv = (coefs[j, k] for k in range(3))
        new = tuple(f * inv - ai * y - ri * x for f, x, y in zip(rhs(j), one, two))
        for number in range(5):
            values[j, number] = new[number]
        return (new, one)

    rows_loop(ROWS, row, ((zero,) * 5, (zero,) * 5))


def backward_values(coefs, values):
    zero = jnp.zeros((8, 128), jnp.float32)

    def row(i, carry):
        j = ROWS - 1 - i
        one, two = carry
        p, q = coefs[j, 3], coefs[j, 4]
        new = tuple(values[j, v] - p * one[v] - q * two[v] for v in range(5))
        for number in range(5):
            values[j, number] = new[number]
        return (new, one)

    rows_loop(ROWS, row, ((zero,) * 5, (zero,) * 5))


def finish_values(values, spikes, tails, heads, put):
    def row(j, carry):
        l0, l1, r0, r1 = (spikes[j, k] for k in range(4))
        for v in range(5):
            put(
                j,
                v,
                values[j, v]
                - (l0 * tails[0][v] + l1 * tails[1][v])
                - (r0 * heads[0][v] + r1 * heads[1][v]),
            )
        return carry

    rows_loop(ROWS, row, 0)


def end_spikes(spikes):
    low, high = (0, 1), (ROWS - 2, ROWS - 1)
    take = lambda rows, first: tuple(spikes[r, first + c] for r in rows for c in range(2))
    return take(low, 0), take(high, 0), take(low, 2), take(high, 2)


def chain_factor(count, matrices):
    factors = []
    beta = None
    for i in range(count):
        lh, lt, rh, rt = matrices(i)
        if i == 0:
            factors.append((None, None, None, None, rh, rt))
            beta = rt
            continue
        m = one_minus_inverse(mm(lh, beta))
        delta = mm(m, rh)
        ltb = mm(lt, beta)
        beta = plus(rt, mm(ltb, delta))
        factors.append((lh, lt, m, ltb, delta, beta))
    return factors


def chain_values(count, factors, ends):
    gammas, alphas = [], []
    for i in range(count):
        gh, gt = ends(i)
        if i:
            lh, lt, m, ltb = factors[i][:4]
            alpha = alphas[-1]
            gh = mv(m, minus(gh, mv(lh, alpha)))
            gt = plus(minus(gt, mv(lt, alpha)), mv(ltb, gh))
        gammas.append(gh)
        alphas.append(gt)
    heads, tails = [None] * count, [None] * count
    heads[-1], tails[-1] = gammas[-1], alphas[-1]
    for i in range(count - 2, -1, -1):
        heads[i] = minus(gammas[i], mv(factors[i][4], heads[i + 1]))
        tails[i] = minus(alphas[i], mv(factors[i][5], heads[i + 1]))
    return heads, tails


def merge_matrices(left, right):
    lha, lta, rha, rta = left
    lhb, ltb, rhb, rtb = right
    n = one_minus_inverse(mm(rta, lhb))
    l_tau = mm(n, lta)
    r_tau = negative(mm(n, mm(rta, rhb)))
    l_eta = negative(mm(lhb, l_tau))
    r_eta = minus(rhb, mm(lhb, r_tau))
    lh = minus(lha, mm(rha, l_eta))
    rh = negative(mm(rha, r_eta))
    lt = negative(mm(ltb, l_tau))
    rt = minus(rtb, mm(ltb, r_tau))
    use = (n, rta, lhb, rha, ltb, l_tau, r_tau, l_eta, r_eta)
    return (lh, lt, rh, rt), use


def merge_values(use, gha, gta, ghb, gtb):
    n, rta, lhb, rha, ltb = use[:5]
    tau = mv(n, minus(gta, mv(rta, ghb)))
    eta = minus(ghb, mv(lhb, tau))
    return minus(gha, mv(rha, eta)), minus(gtb, mv(ltb, tau)), tau, eta


def split_values(use, tau, eta, tail, head):
    l_tau, r_tau, l_eta, r_eta = use[5:]
    inner_tail = minus(minus(tau, mv(l_tau, tail)), mv(r_tau, head))
    inner_head = minus(minus(eta, mv(l_eta, tail)), mv(r_eta, head))
    return inner_tail, inner_head


def up(items, amount):
    return tuple(pltpu.roll(x, 8 - amount, 0) for x in items)


def down(items, amount):
    return tuple(pltpu.roll(x, amount, 0) for x in items)


def flipped(index, mask):
    result, bit = index, 1
    while bit <= mask:
        if mask & bit:
            result = result + bit - 2 * bit * lax.rem(index // bit, 2)
        bit *= 2
    return result


def kernel(
    gy, gz, state_h, conduct_h, yb_h, zb_h, zval, zspike, ends_ref,
    yb, zb, field, zsend, zrecv,
    ycoef, yspike, yval, zcoef, zbt, yplane, plane,
    ym_out, ym_in, yv_out, yv_in, yr_out, yr_in, zm_all, zv_all, ht_all,
    in_sem, yh_s, yh_r, zh_s, zh_r, ym_s, ym_r, yv_s, yv_r, yr_s, yr_r,
    zm_s, zm_r, zv_s, zv_r, own_sem,
):
    me, mz = lax.axis_index("gy"), lax.axis_index("gz")
    step = gy // 8
    lanes = lax.broadcasted_iota(jnp.int32, (8, 128), 1)
    subs = lax.broadcasted_iota(jnp.int32, (8, 128), 0)
    seg = lax.rem(subs, 4)
    zero = jnp.zeros((8, 128), jnp.float32)

    inside = pl.ds(1, ROWS)
    loads = [
        [pltpu.make_async_copy(src.at[x], dst(x), in_sem.at[k, x]) for x in range(8)]
        for k, (src, dst) in enumerate(
            (
                (state_h, lambda x: field.at[pl.ds(0, 5), inside, x]),
                (conduct_h, lambda x: field.at[5, inside, x]),
                (yb_h, lambda x: yb.at[:, :, x]),
                (zb_h, lambda x: zb.at[:, :, x]),
            )
        )
    ]
    for load in loads:
        for copy in load:
            copy.start()

    def loaded(k):
        for copy in loads[k]:
            copy.wait()

    barrier = pltpu.get_barrier_semaphore()
    for k in range(1, gy):
        pl.semaphore_signal(
            barrier, inc=1, device_id=(lax.rem(me + k, gy), mz), device_id_type=MESH
        )
    for k in range(1, gz):
        pl.semaphore_signal(
            barrier, inc=1, device_id=(me, lax.rem(mz + k, gz)), device_id_type=MESH
        )

    loaded(0)
    loaded(1)

    def pack_row(j, carry):
        a0, a1, b0, b1 = carry
        for v in range(6):
            tile = field[v, j + 1]
            place = (v % 4) * ROWS + j
            moved = pltpu.roll(tile, (place + 1) % 128, 1)
            at_a = lanes == place
            at_b = lanes == (place + 1) % 128
            if v < 4:
                a0, b0 = jnp.where(at_a, moved, a0), jnp.where(at_b, moved, b0)
            else:
                a1, b1 = jnp.where(at_a, moved, a1), jnp.where(at_b, moved, b1)
        return (a0, a1, b0, b1)

    a0, a1, b0, b1 = rows_loop(ROWS, pack_row, (zero,) * 4)
    zsend[0, 0], zsend[0, 1], zsend[1, 0], zsend[1, 1] = a0, a1, b0, b1
    pl.semaphore_wait(barrier, gy + gz - 2)

    def remote(src, dst, send, recv, there):
        return pltpu.make_async_remote_copy(
            src_ref=src, dst_ref=dst, send_sem=send, recv_sem=recv,
            device_id=there, device_id_type=MESH,
        )

    prev_y, next_y = lax.rem(me + gy - 1, gy), lax.rem(me + 1, gy)
    prev_z, next_z = lax.rem(mz + gz - 1, gz), lax.rem(mz + 1, gz)
    z_fwd = remote(zsend.at[0], zrecv.at[0], zh_s.at[0], zh_r.at[0], (me, next_z))
    z_bwd = remote(zsend.at[1], zrecv.at[1], zh_s.at[1], zh_r.at[1], (me, prev_z))
    y_fwd = remote(field.at[:, ROWS], field.at[:, 0], yh_s.at[0], yh_r.at[0], (next_y, mz))
    y_bwd = remote(field.at[:, 1], field.at[:, ROWS + 1], yh_s.at[1], yh_r.at[1], (prev_y, mz))
    pl.when(mz < gz - 1)(z_fwd.start)
    pl.when(mz > 0)(z_bwd.start)
    pl.when(me < gy - 1)(y_fwd.start)
    pl.when(me > 0)(y_bwd.start)

    @pl.when(mz == 0)
    def _():
        zrecv[0] = jnp.zeros((2, 8, 128), jnp.float32)

    @pl.when(mz == gz - 1)
    def _():
        zrecv[1] = jnp.zeros((2, 8, 128), jnp.float32)

    @pl.when(me == 0)
    def _():
        field[:, 0] = jnp.zeros((6, 8, 128), jnp.float32)

    @pl.when(me == gy - 1)
    def _():
        field[:, ROWS + 1] = jnp.zeros((6, 8, 128), jnp.float32)

    loaded(2)
    factor_segment(
        lambda k, j: yb[k, j], ycoef, yspike
    )
    for number, item in enumerate(sum(end_spikes(yspike), ())):
        ym_out[number] = item

    place_of_mine = me // step
    owner = lax.rem(me, step) == 0

    def scatter(out, into, rows, send, recv, own, finish):
        for k in (6, 7, 4, 5, 2, 3, 1, 0):
            x = flipped(place_of_mine, k)
            source = out.at[:, x]
            target = into.at[me]
            away = remote(source, target, send.at[k], recv.at[me], (x * step, mz))
            here = pltpu.make_async_copy(source, target, own)
            act = (lambda c: c.wait_send()) if finish else (lambda c: c.start())
            if k:
                act(away)
            else:
                if step > 1:
                    pl.when(jnp.logical_not(owner))(lambda: act(away))
                local = here.wait if finish else here.start
                pl.when(owner)(local) if step > 1 else local()

    def scatter_arrived(out, into, rows, send, recv):
        for k in range(1, gy):
            i = lax.rem(me + k, gy)
            source = out.at[:, 0]
            target = into.at[i]
            remote(source, target, send.at[0], recv.at[i], (i, mz)).wait_recv()

    scatter(ym_out, ym_in, 16, ym_s, ym_r, own_sem.at[0], False)

    @pl.when(mz > 0)
    def _():
        z_fwd.wait_recv()

    @pl.when(mz < gz - 1)
    def _():
        z_bwd.wait_recv()

    @pl.when(me > 0)
    def _():
        y_fwd.wait_recv()

    @pl.when(me < gy - 1)
    def _():
        y_bwd.wait_recv()

    def shifted(j, v):
        tile = field[v, j + 1]
        place = (v % 4) * ROWS + j
        low = pltpu.roll(zrecv[0, v // 4], (128 - place) % 128, 1)
        high = pltpu.roll(zrecv[1, v // 4], (254 - place) % 128, 1)
        before = jnp.where(lanes == 0, low, pltpu.roll(tile, 1, 1))
        after = jnp.where(lanes == 127, high, pltpu.roll(tile, 127, 1))
        return tile, before, after

    def flux_rhs(j):
        k_here, k_before, k_after = shifted(j, 5)
        north = flux_tenth * (k_here + field[5, j + 2])
        south = flux_tenth * (k_here + field[5, j])
        upward = flux_tenth * (k_here + k_after)
        downward = flux_tenth * (k_here + k_before)
        result = []
        for v in range(5):
            here, before, after = shifted(j, v)
            result.append(
                here
                + (north * (field[v, j + 2] - here) - south * (here - field[v, j]))
                + (upward * (after - here) - downward * (here - before))
            )
        return result

    forward_values(flux_rhs, ycoef, yval)
    backward_values(ycoef, yval)
    for number, r in enumerate((0, 1, ROWS - 2, ROWS - 1)):
        for v in range(5):
            yv_out[5 * number + v] = yval[r, v]
    scatter(yv_out, yv_in, PACK, yv_s, yv_r, own_sem.at[1], False)

    loaded(3)

    def turn(source, target, k):
        for g in range(2):
            turned = source[k, pl.ds(g * HALF, HALF)].reshape(128, 128).T
            for part in range(4):
                rows = turned[part * ROWS : (part + 1) * ROWS]
                target[k, pl.ds((4 * g + part) * STEP, ROWS), :] = rows

    for k in range(5):
        turn(zb, zbt, k)
    scatter_done = functools.partial(scatter, finish=True)

    def owner_solve():
        scatter_arrived(ym_out, ym_in, 16, ym_s, ym_r)

        def matrices(i):
            rows = [
                jnp.broadcast_to(ym_in[i, pl.ds(q, 1), :], (8, 128)) for q in range(16)
            ]
            return tuple(tuple(rows[4 * b : 4 * b + 4]) for b in range(4))

        factors = chain_factor(gy, matrices)
        scatter_arrived(yv_out, yv_in, PACK, yv_s, yv_r)

        def ends(i):
            parts = [yv_in[i, pl.ds(5 * q, 5), :] for q in range(4)]
            parts = [jnp.concatenate([x, jnp.zeros((3, 128), jnp.float32)], axis=0) for x in parts]
            return (parts[0], parts[1]), (parts[2], parts[3])

        heads, tails = chain_values(gy, factors, ends)
        for i in range(gy):
            before = tails[i - 1] if i else (zero, zero)
            behind = heads[i + 1] if i < gy - 1 else (zero, zero)
            for q, item in enumerate(before + behind):
                yr_out[i, pl.ds(5 * q, 5), :] = item[0:5]

    def ret(k):
        i = flipped(me, k)
        source = yr_out.at[i]
        target = yr_in.at[:, place_of_mine]
        return source, target, i

    def owner_part():
        scatter_done(ym_out, ym_in, 16, ym_s, ym_r, own_sem.at[0]) if step == 1 else None
        scatter_done(yv_out, yv_in, PACK, yv_s, yv_r, own_sem.at[1]) if step == 1 else None
        owner_solve()
        for k in sorted(range(1, gy), key=lambda k: (6, 7, 4, 5, 2, 3, 1).index(k) if k < 8 else -k):
            source, target, i = ret(k)
            remote(source, target, yr_s.at[k], yr_r.at[place_of_mine], (i, mz)).start()
        source, target, i = ret(0)
        pltpu.make_async_copy(source, target, own_sem.at[2]).start()

    if step > 1:
        scatter_done(ym_out, ym_in, 16, ym_s, ym_r, own_sem.at[0])
        scatter_done(yv_out, yv_in, PACK, yv_s, yv_r, own_sem.at[1])
        pl.when(owner)(owner_part)
    else:
        owner_part()

    factor_segment(lambda k, j: zbt[k, pl.ds(j, 8, stride=STEP), :], zcoef, zspike)
    level_0 = end_spikes(zspike)
    level_1, use_1 = merge_matrices(level_0, tuple(up(m, 1) for m in level_0))
    level_2, use_2 = merge_matrices(level_1, tuple(up(m, 2) for m in level_1))

    def pack_four(tiles):
        packed = tiles[0]
        for k in range(1, 4):
            packed = jnp.where(seg == k, pltpu.roll(tiles[k], k, 0), packed)
        return packed

    def partners(act):
        for away in range(gz - 1, 0, -1):
            pl.when(mz + away < gz)(functools.partial(act, mz + away))
            pl.when(mz - away >= 0)(functools.partial(act, mz - away))

    def gather(ref, send, recv):
        def act(there):
            remote(ref.at[mz], ref.at[mz], send.at[there], recv.at[mz], (me, there)).start()

        partners(act)

    def gathered(ref, send, recv):
        def act(there):
            remote(ref.at[mz], ref.at[there], send.at[there], recv.at[there], (me, there)).wait_recv()

        partners(act)

    def gather_sent(ref, send, recv):
        def act(there):
            remote(ref.at[mz], ref.at[mz], send.at[there], recv.at[mz], (me, there)).wait_send()

        partners(act)

    for b in range(4):
        zm_all[mz, b] = pack_four(level_2[b])
    gather(zm_all, zm_s, zm_r)

    def y_returned():
        for k in range(8):
            x = flipped(place_of_mine, k)
            target = yr_in.at[:, x]
            away = remote(yr_out.at[0], target, yr_s.at[0], yr_r.at[x], (x * step, mz))
            here = pltpu.make_async_copy(yr_out.at[0], target, own_sem.at[2])
            if k:
                away.wait_recv()
            elif step > 1:
                pl.when(jnp.logical_not(owner))(away.wait_recv)
                pl.when(owner)(here.wait)
            else:
                here.wait()

    y_returned()
    got = [[yr_in[5 * q + v] for v in range(5)] for q in range(4)]

    def put_y(j, v, tile):
        yplane[v, j] = tile

    finish_values(yval, yspike, got[:2], got[2:], put_y)
    for v in range(5):
        turn(yplane, plane, v)

    forward_values(
        lambda j: [plane[v, pl.ds(j, 8, stride=STEP), :] for v in range(5)], zcoef, zval
    )
    backward_values(zcoef, zval)
    merged = []
    for v in range(5):
        gh = (zval[0, v], zval[1, v])
        gt = (zval[ROWS - 2, v], zval[ROWS - 1, v])
        gh1, gt1, tau1, eta1 = merge_values(use_1, gh, gt, up(gh, 1), up(gt, 1))
        gh2, gt2, tau2, eta2 = merge_values(use_2, gh1, gt1, up(gh1, 2), up(gt1, 2))
        merged.append((gh2 + gt2, tau1, eta1, tau2, eta2))
    for q in range(4):
        zv_all[mz, q] = pack_four([merged[v][0][q] for v in range(4)])
    zv_all[mz, 4] = pack_four([merged[4][0][q] for q in range(4)])
    gather(zv_all, zv_s, zv_r)

    gathered(zm_all, zm_s, zm_r)

    def spread(tile, k):
        result = tile
        for r in range(4):
            if r != k:
                result = jnp.where(seg == r, pltpu.roll(tile, (r - k) % 8, 0), result)
        return result

    def z_matrices(i):
        return tuple(tuple(spread(zm_all[i, b], k) for k in range(4)) for b in range(4))

    factors = chain_factor(gz, z_matrices)
    gathered(zv_all, zv_s, zv_r)

    def z_ends(i):
        return (zv_all[i, 0], zv_all[i, 1]), (zv_all[i, 2], zv_all[i, 3])

    def z_ends_last(i):
        tiles = [pltpu.roll(zv_all[i, 4], (8 - q) % 8, 0) if q else zv_all[i, 4] for q in range(4)]
        return (tiles[0], tiles[1]), (tiles[2], tiles[3])

    for number, ends in enumerate((z_ends, z_ends_last)):
        heads, tails = chain_values(gz, factors, ends)
        for i in range(gz):
            before = tails[i - 1] if i else (zero, zero)
            behind = heads[i + 1] if i < gz - 1 else (zero, zero)
            for q, item in enumerate(before + behind):
                ht_all[i, 4 * number + q] = item
    tails_in, heads_in = [[], []], [[], []]
    for v in range(5):
        base, shift = (0, v) if v < 4 else (4, 0)
        outer = tuple(ht_all[mz, base + q] for q in range(4))
        outer = up(outer, shift) if shift else outer
        tail, head = outer[:2], outer[2:]
        _, tau1, eta1, tau2, eta2 = merged[v]
        tail2, head2 = split_values(use_2, tau2, eta2, tail, head)
        tail_d, head_d = down(tail2, 2), down(head, 2)
        tail1 = tuple(jnp.where(seg == 2, d, t) for d, t in zip(tail_d, tail))
        head1 = tuple(jnp.where(seg == 2, d, h) for d, h in zip(head_d, head2))
        inner_t, inner_h = split_values(use_1, tau1, eta1, tail1, head1)
        odd = lax.rem(seg, 2) == 1
        for q in range(2):
            tails_in[q].append(jnp.where(odd, down(inner_t, 1)[q], tail1[q]))
            heads_in[q].append(jnp.where(odd, down(head1, 1)[q], inner_h[q]))

    for q in range(2):
        for v in range(5):
            ends_ref[q * 5 + v] = tails_in[q][v]
            ends_ref[10 + q * 5 + v] = heads_in[q][v]

    pl.when(mz < gz - 1)(z_fwd.wait_send)
    pl.when(mz > 0)(z_bwd.wait_send)
    pl.when(me < gy - 1)(y_fwd.wait_send)
    pl.when(me > 0)(y_bwd.wait_send)

    def returns_sent():
        for k in range(1, gy):
            source, target, i = ret(k)
            remote(source, target, yr_s.at[k], yr_r.at[place_of_mine], (i, mz)).wait_send()

    pl.when(owner)(returns_sent) if step > 1 else returns_sent()
    gather_sent(zm_all, zm_s, zm_r)
    gather_sent(zv_all, zv_s, zv_r)


def last_kernel(zval, zspike, ends, out, plane, block, sems):
    copies = []
    for v in range(5):
        t0, t1, h0, h1 = (ends[q * 5 + v] for q in range(4))
        for j in range(ROWS):
            l0, l1, r0, r1 = (zspike[j, q] for q in range(4))
            plane[v, pl.ds(j, 8, stride=STEP), :] = (
                zval[j, v] - (l0 * t0 + l1 * t1) - (r0 * h0 + r1 * h1)
            )
        for g in range(2):
            parts = [plane[v, pl.ds((4 * g + part) * STEP, ROWS), :] for part in range(4)]
            turned = jnp.concatenate(parts, axis=0).T
            block[v, pl.ds(g * HALF, HALF)] = turned.reshape(HALF, 8, 128)
        for x in range(8):
            copies.append(
                pltpu.make_async_copy(
                    block.at[v, :, x], out.at[x, pl.ds(v * ROWS, ROWS)], sems.at[v, x]
                )
            )
            copies[-1].start()
    for copy in copies:
        copy.wait()


def solution(mesh):
    gy, gz = mesh.shape["gy"], mesh.shape["gz"]
    assert gy % 8 == 0
    spec = P(None, None, "gy", "gz")

    def per_device(state, conduct, y_bands, z_bands):
        assert state.shape == (8, 5, ROWS, 128)
        tile = lambda *lead: pltpu.VMEM((*lead, 8, 128), jnp.float32)
        flat = lambda *shape: pltpu.VMEM((*shape, 128), jnp.float32)
        dma = lambda *count: pltpu.SemaphoreType.DMA(count)
        inner = pl.pallas_call(
            functools.partial(kernel, gy, gz),
            out_shape=[tile(ROWS, 5), tile(ROWS, 4), tile(20)],
            in_specs=[pl.BlockSpec(memory_space=pl.ANY)] * 4,
            out_specs=[pl.BlockSpec(memory_space=pltpu.VMEM)] * 3,
            scratch_shapes=[
                tile(5, ROWS), tile(5, ROWS), tile(6, ROWS + 2), tile(2, 2), tile(2, 2),
                tile(ROWS, 5), tile(ROWS, 4), tile(ROWS, 5),
                tile(ROWS, 5),
                flat(5, 8 * STEP), tile(5, ROWS), flat(5, 8 * STEP),
                tile(16), flat(gy, 16), tile(PACK), flat(gy, PACK),
                flat(gy, PACK), tile(PACK),
                tile(gz, 4), tile(gz, 5), tile(gz, 8),
                dma(4, 8), dma(2), dma(2), dma(2), dma(2),
                dma(8), dma(gy), dma(8), dma(gy), dma(gy), dma(8),
                dma(gz), dma(gz), dma(gz), dma(gz), dma(3),
            ],
            compiler_params=pltpu.CompilerParams(collective_id=0, has_side_effects=True),
        )(
            state, conduct, y_bands, z_bands,
        )
        result = pl.pallas_call(
            last_kernel,
            out_shape=jax.ShapeDtypeStruct((8, 5 * ROWS, 128), jnp.float32),
            in_specs=[pl.BlockSpec(memory_space=pltpu.VMEM)] * 3,
            out_specs=pl.BlockSpec(memory_space=pl.ANY),
            scratch_shapes=[flat(5, 8 * STEP), tile(5, ROWS), dma(5, 8)],
        )(*(pltpu.with_memory_space_constraint(x, pltpu.MemorySpace.VMEM) for x in inner))
        return result.reshape(state.shape)

    return jax.shard_map(
        per_device, mesh=mesh, in_specs=(spec, P(None, "gy", "gz"), spec, spec),
        out_specs=spec, check_vma=False,
    )
```

profile of v0, /device:TPU:0, one launch (start us, length us, event | category | flops | bytes accessed | tf_op | source)
XLA Modules:
  0.0 22.6 jit_solution(10975350006691701791)
XLA Ops:
  0.0 21.3 %shard_map.46 = (f32[32,5,8,128]{3,2,1,0:T(8,128)S(1)}, f32[32,4,8,128]{3,2,1,0:T(8,128)S(1)}, f32[20,8,128]{2,1,0:T(8,128)S(1)}) custom-call(f32[8,5,32,128]{3,2,1,0:T(8,128)} %state_h.1, f32[8,32,128]{2,1,0:T(8,128)} %conduct_h.1, f32[8,5,32,128]{3,2,1,0:T(8,128)} %yb_h.1, f32[8,5,32,128]{3,2,1,0:T(8,128)} %zb_h.1), custom_call_target="tpu_custom_call" | custom-call | tf_op jit(solution)/shard_map/pallas_call | solution.py:661
  21.3 1.3 %shard_map.47 = f32[8,160,128]{2,1,0:T(8,128)} custom-call(f32[32,5,8,128]{3,2,1,0:T(8,128)S(1)} %get-tuple-element.8.zval, f32[32,4,8,128]{3,2,1,0:T(8,128)S(1)} %get-tuple-element.9.zspike, f32[20,8,128]{2,1,0:T(8,128)S(1)} %get-tuple-element.10.ends), custom_call_target="tpu_custom_call" | custom-call | tf_op jit(solution)/shard_map/pallas_call | solution.py:682
where the time goes:
time: 22.8 us; the launch traced here: 22.6 us
  Pallas kernels  22.6 us (99%)
    pallas_call x1, Pallas kernels, per_device(): pl.pallas_call(functools.partial(kernel, gy, gz), out_shape=[tile(ROWS, 5...  21.3 us
    pallas_call x1, Pallas kernels, per_device(): pl.pallas_call(last_kernel, out_shape=jax.ShapeDtypeStruct((8, 5 * ROWS,...  1.32 us

commit v1 on v0

--- a/solution.py
+++ b/solution.py
@@ -11,6 +11,7 @@
 MESH = pl.DeviceIdType.MESH
 ROWS = 32
 PACK = 20
+EDGE = 32
 STEP = ROWS + 1
 HALF = ROWS // 2
 
@@ -60,7 +61,7 @@
     return (m11 * scale, -m01 * scale, -m10 * scale, m00 * scale)
 
 
-def factor_segment(band, coefs, spikes):
+def factor_segment(band, coefs, spikes, unit=False):
     zero = jnp.zeros((8, 128), jnp.float32)
 
     def one_row(j, carry, left):
@@ -73,7 +74,7 @@
         ai = a * inv
         ri = red * inv
         if left == 0:
-            l0, l1 = ai, b * inv
+            l0, l1 = (inv if unit else ai), b * inv
         elif left == 1:
             l0, l1 = -ri * l01, ai - ri * l11
         else:
@@ -94,14 +95,16 @@
         j = ROWS - 1 - i
         one, two = carry
         p, q = coefs[j, 3], coefs[j, 4]
-        start = (spikes[j, 0], spikes[j, 1], zero, zero)
+        last = coefs[j, 2] if unit and i == 0 else zero
+        start = (spikes[j, 0], spikes[j, 1], zero, last)
         new = tuple(s - p * x - q * y for s, x, y in zip(start, one, two))
         for number in range(4):
             spikes[j, number] = new[number]
         return (new, one)
 
     minus_one = zero - 1.0
-    rows_loop(ROWS, back, ((zero, zero, minus_one, zero), (zero, zero, zero, minus_one)))
+    beyond = zero if unit else minus_one
+    rows_loop(ROWS, back, ((zero, zero, minus_one, zero), (zero, zero, zero, beyond)))
 
 
 def forward_values(rhs, coefs, values):
@@ -243,7 +246,7 @@
     yb, zb, field, zsend, zrecv,
     ycoef, yspike, yval, zcoef, zbt, yplane, plane,
     ym_out, ym_in, yv_out, yv_in, yr_out, yr_in, zm_all, zv_all, ht_all,
-    in_sem, yh_s, yh_r, zh_s, zh_r, ym_s, ym_r, yv_s, yv_r, yr_s, yr_r,
+    in_sem, zh_s, zh_r, ym_s, ym_r, yv_s, yv_r, yr_s, yr_r,
     zm_s, zm_r, zv_s, zv_r, own_sem,
 ):
     me, mz = lax.axis_index("gy"), lax.axis_index("gz")
@@ -253,13 +256,12 @@
     seg = lax.rem(subs, 4)
     zero = jnp.zeros((8, 128), jnp.float32)
 
-    inside = pl.ds(1, ROWS)
     loads = [
         [pltpu.make_async_copy(src.at[x], dst(x), in_sem.at[k, x]) for x in range(8)]
         for k, (src, dst) in enumerate(
             (
-                (state_h, lambda x: field.at[pl.ds(0, 5), inside, x]),
-                (conduct_h, lambda x: field.at[5, inside, x]),
+                (state_h, lambda x: field.at[pl.ds(0, 5), :, x]),
+                (conduct_h, lambda x: field.at[5, :, x]),
                 (yb_h, lambda x: yb.at[:, :, x]),
                 (zb_h, lambda x: zb.at[:, :, x]),
             )
@@ -289,7 +291,7 @@
     def pack_row(j, carry):
         a0, a1, b0, b1 = carry
         for v in range(6):
-            tile = field[v, j + 1]
+            tile = field[v, j]
             place = (v % 4) * ROWS + j
             moved = pltpu.roll(tile, (place + 1) % 128, 1)
             at_a = lanes == place
@@ -310,16 +312,11 @@
             device_id=there, device_id_type=MESH,
         )
 
-    prev_y, next_y = lax.rem(me + gy - 1, gy), lax.rem(me + 1, gy)
     prev_z, next_z = lax.rem(mz + gz - 1, gz), lax.rem(mz + 1, gz)
     z_fwd = remote(zsend.at[0], zrecv.at[0], zh_s.at[0], zh_r.at[0], (me, next_z))
     z_bwd = remote(zsend.at[1], zrecv.at[1], zh_s.at[1], zh_r.at[1], (me, prev_z))
-    y_fwd = remote(field.at[:, ROWS], field.at[:, 0], yh_s.at[0], yh_r.at[0], (next_y, mz))
-    y_bwd = remote(field.at[:, 1], field.at[:, ROWS + 1], yh_s.at[1], yh_r.at[1], (prev_y, mz))
     pl.when(mz < gz - 1)(z_fwd.start)
     pl.when(mz > 0)(z_bwd.start)
-    pl.when(me < gy - 1)(y_fwd.start)
-    pl.when(me > 0)(y_bwd.start)
 
     @pl.when(mz == 0)
     def _():
@@ -329,25 +326,20 @@
     def _():
         zrecv[1] = jnp.zeros((2, 8, 128), jnp.float32)
 
-    @pl.when(me == 0)
-    def _():
-        field[:, 0] = jnp.zeros((6, 8, 128), jnp.float32)
-
-    @pl.when(me == gy - 1)
-    def _():
-        field[:, ROWS + 1] = jnp.zeros((6, 8, 128), jnp.float32)
-
     loaded(2)
     factor_segment(
-        lambda k, j: yb[k, j], ycoef, yspike
+        lambda k, j: yb[k, j], ycoef, yspike, True
     )
-    for number, item in enumerate(sum(end_spikes(yspike), ())):
+    sent = list(sum(end_spikes(yspike), ())) + [yb[0, 0], yb[4, ROWS - 1]]
+    for j in (ROWS - 1, 0):
+        sent += [field[v, j] for v in range(6)]
+    for number, item in enumerate(sent + [zero, zero]):
         ym_out[number] = item
 
     place_of_mine = me // step
     owner = lax.rem(me, step) == 0
 
-    def scatter(out, into, rows, send, recv, own, finish):
+    def scatter(out, into, send, recv, own, finish):
         for k in (6, 7, 4, 5, 2, 3, 1, 0):
             x = flipped(place_of_mine, k)
             source = out.at[:, x]
@@ -363,14 +355,33 @@
                 local = here.wait if finish else here.start
                 pl.when(owner)(local) if step > 1 else local()
 
-    def scatter_arrived(out, into, rows, send, recv):
+    def scatter_arrived(out, into, send, recv):
         for k in range(1, gy):
             i = lax.rem(me + k, gy)
             source = out.at[:, 0]
             target = into.at[i]
             remote(source, target, send.at[0], recv.at[i], (i, mz)).wait_recv()
 
-    scatter(ym_out, ym_in, 16, ym_s, ym_r, own_sem.at[0], False)
+    scatter(ym_out, ym_in, ym_s, ym_r, own_sem.at[0], False)
+
+    first_lane, last_lane = lanes == 0, lanes == 127
+    slot = lanes // ROWS
+
+    def own_flux(j, carry):
+        k = field[5, j]
+        along = jnp.where(last_lane, zero, flux_tenth * (k + pltpu.roll(k, 127, 1)))
+        across = flux_tenth * (k + field[5, j + 1]) if j < ROWS - 1 else zero
+        new = []
+        for v in range(5):
+            here = field[v, j]
+            z_flow = along * (pltpu.roll(here, 127, 1) - here)
+            y_flow = across * (field[v, j + 1] - here) if j < ROWS - 1 else zero
+            y_part = y_flow - carry[v] if 0 < j < ROWS - 1 else (y_flow if j == 0 else -carry[v])
+            yval[j, v] = here + (y_part + (z_flow - pltpu.roll(z_flow, 1, 1)))
+            new.append(y_flow)
+        return tuple(new)
+
+    rows_loop(ROWS, own_flux, (zero,) * 5)
 
     @pl.when(mz > 0)
     def _():
@@ -380,37 +391,25 @@
     def _():
         z_bwd.wait_recv()
 
-    @pl.when(me > 0)
-    def _():
-        y_fwd.wait_recv()
-
-    @pl.when(me < gy - 1)
-    def _():
-        y_bwd.wait_recv()
-
-    def shifted(j, v):
-        tile = field[v, j + 1]
-        place = (v % 4) * ROWS + j
-        low = pltpu.roll(zrecv[0, v // 4], (128 - place) % 128, 1)
-        high = pltpu.roll(zrecv[1, v // 4], (254 - place) % 128, 1)
-        before = jnp.where(lanes == 0, low, pltpu.roll(tile, 1, 1))
-        after = jnp.where(lanes == 127, high, pltpu.roll(tile, 127, 1))
-        return tile, before, after
+    def edge_flux(theirs, ours):
+        both = theirs[1] + ours[1]
+        k = jnp.where(slot == 0, pltpu.roll(both, 96, 1), both)
+        k = jnp.where(slot == 2, pltpu.roll(both, 32, 1), k)
+        k = jnp.where(slot == 3, pltpu.roll(both, 64, 1), k)
+        return [flux_tenth * k * (x - y) for x, y in zip(theirs, ours)]
+
+    back_one = lambda tiles: [pltpu.roll(t, 127, 1) for t in tiles]
+    low = edge_flux([zrecv[0, 0], zrecv[0, 1]], back_one((b0, b1)))
+    high = back_one(edge_flux(back_one((zrecv[1, 0], zrecv[1, 1])), (a0, a1)))
+    edge = jnp.logical_or(first_lane, last_lane)
 
     def flux_rhs(j):
-        k_here, k_before, k_after = shifted(j, 5)
-        north = flux_tenth * (k_here + field[5, j + 2])
-        south = flux_tenth * (k_here + field[5, j])
-        upward = flux_tenth * (k_here + k_after)
-        downward = flux_tenth * (k_here + k_before)
         result = []
         for v in range(5):
-            here, before, after = shifted(j, v)
-            result.append(
-                here
-                + (north * (field[v, j + 2] - here) - south * (here - field[v, j]))
-                + (upward * (after - here) - downward * (here - before))
-            )
+            place = (v % 4) * ROWS + j
+            added = jnp.where(lanes == place, low[v // 4], high[v // 4])
+            added = pltpu.roll(added, 128 - place, 1) if place else added
+            result.append(yval[j, v] + jnp.where(edge, added, zero))
         return result
 
     forward_values(flux_rhs, ycoef, yval)
@@ -418,7 +417,7 @@
     for number, r in enumerate((0, 1, ROWS - 2, ROWS - 1)):
         for v in range(5):
             yv_out[5 * number + v] = yval[r, v]
-    scatter(yv_out, yv_in, PACK, yv_s, yv_r, own_sem.at[1], False)
+    scatter(yv_out, yv_in, yv_s, yv_r, own_sem.at[1], False)
 
     loaded(3)
 
@@ -434,27 +433,49 @@
     scatter_done = functools.partial(scatter, finish=True)
 
     def owner_solve():
-        scatter_arrived(ym_out, ym_in, 16, ym_s, ym_r)
+        scatter_arrived(ym_out, ym_in, ym_s, ym_r)
+
+        wide = lambda i, q: jnp.broadcast_to(ym_in[i, pl.ds(q, 1), :], (8, 128))
+        rows = [[wide(i, q) for q in range(18)] for i in range(gy)]
 
         def matrices(i):
-            rows = [
-                jnp.broadcast_to(ym_in[i, pl.ds(q, 1), :], (8, 128)) for q in range(16)
-            ]
-            return tuple(tuple(rows[4 * b : 4 * b + 4]) for b in range(4))
-
+            a, e = rows[i][16:]
+            lh, lt = ((g[0] * a, g[1], g[2] * a, g[3]) for g in (rows[i][:4], rows[i][4:8]))
+            rh, rt = ((g[0], g[1] * e, g[2], g[3] * e) for g in (rows[i][8:12], rows[i][12:16]))
+            return lh, lt, rh, rt
+
+        def edges(i, first):
+            if not 0 <= i < gy:
+                return zero, zero
+            return ym_in[i, pl.ds(first, 8), :], wide(i, first + 5)
+
+        flows = []
+        for i in range(gy + 1):
+            (s_last, k_last), (s_first, k_first) = edges(i - 1, 18), edges(i, 24)
+            flows.append(flux_tenth * (k_last + k_first) * (s_first - s_last))
         factors = chain_factor(gy, matrices)
-        scatter_arrived(yv_out, yv_in, PACK, yv_s, yv_r)
+        added = [
+            [rows[i][q + 9] * flows[i + 1] - rows[i][q] * flows[i] for q in (0, 2, 4, 6)]
+            for i in range(gy)
+        ]
+        scatter_arrived(yv_out, yv_in, yv_s, yv_r)
 
         def ends(i):
             parts = [yv_in[i, pl.ds(5 * q, 5), :] for q in range(4)]
             parts = [jnp.concatenate([x, jnp.zeros((3, 128), jnp.float32)], axis=0) for x in parts]
+            parts = plus(parts, added[i])
             return (parts[0], parts[1]), (parts[2], parts[3])
 
         heads, tails = chain_values(gy, factors, ends)
         for i in range(gy):
             before = tails[i - 1] if i else (zero, zero)
             behind = heads[i + 1] if i < gy - 1 else (zero, zero)
-            for q, item in enumerate(before + behind):
+            a, e = rows[i][16:]
+            back = (
+                a * before[0] + flows[i], before[1],
+                behind[0], e * behind[1] - flows[i + 1],
+            )
+            for q, item in enumerate(back):
                 yr_out[i, pl.ds(5 * q, 5), :] = item[0:5]
 
     def ret(k):
@@ -464,8 +485,8 @@
         return source, target, i
 
     def owner_part():
-        scatter_done(ym_out, ym_in, 16, ym_s, ym_r, own_sem.at[0]) if step == 1 else None
-        scatter_done(yv_out, yv_in, PACK, yv_s, yv_r, own_sem.at[1]) if step == 1 else None
+        scatter_done(ym_out, ym_in, ym_s, ym_r, own_sem.at[0]) if step == 1 else None
+        scatter_done(yv_out, yv_in, yv_s, yv_r, own_sem.at[1]) if step == 1 else None
         owner_solve()
         for k in sorted(range(1, gy), key=lambda k: (6, 7, 4, 5, 2, 3, 1).index(k) if k < 8 else -k):
             source, target, i = ret(k)
@@ -474,8 +495,8 @@
         pltpu.make_async_copy(source, target, own_sem.at[2]).start()
 
     if step > 1:
-        scatter_done(ym_out, ym_in, 16, ym_s, ym_r, own_sem.at[0])
-        scatter_done(yv_out, yv_in, PACK, yv_s, yv_r, own_sem.at[1])
+        scatter_done(ym_out, ym_in, ym_s, ym_r, own_sem.at[0])
+        scatter_done(yv_out, yv_in, yv_s, yv_r, own_sem.at[1])
         pl.when(owner)(owner_part)
     else:
         owner_part()
@@ -611,8 +632,6 @@
 
     pl.when(mz < gz - 1)(z_fwd.wait_send)
     pl.when(mz > 0)(z_bwd.wait_send)
-    pl.when(me < gy - 1)(y_fwd.wait_send)
-    pl.when(me > 0)(y_bwd.wait_send)
 
     def returns_sent():
         for k in range(1, gy):
@@ -664,14 +683,14 @@
             in_specs=[pl.BlockSpec(memory_space=pl.ANY)] * 4,
             out_specs=[pl.BlockSpec(memory_space=pltpu.VMEM)] * 3,
             scratch_shapes=[
-                tile(5, ROWS), tile(5, ROWS), tile(6, ROWS + 2), tile(2, 2), tile(2, 2),
+                tile(5, ROWS), tile(5, ROWS), tile(6, ROWS), tile(2, 2), tile(2, 2),
                 tile(ROWS, 5), tile(ROWS, 4), tile(ROWS, 5),
                 tile(ROWS, 5),
                 flat(5, 8 * STEP), tile(5, ROWS), flat(5, 8 * STEP),
-                tile(16), flat(gy, 16), tile(PACK), flat(gy, PACK),
+                tile(EDGE), flat(gy, EDGE), tile(PACK), flat(gy, PACK),
                 flat(gy, PACK), tile(PACK),
                 tile(gz, 4), tile(gz, 5), tile(gz, 8),
-                dma(4, 8), dma(2), dma(2), dma(2), dma(2),
+                dma(4, 8), dma(2), dma(2),
                 dma(8), dma(gy), dma(8), dma(gy), dma(gy), dma(8),
                 dma(gz), dma(gz), dma(gz), dma(gz), dma(3),
             ],

time: 22.8 us -> 22.2 us (0.974)
  Pallas kernels: 22.6 us -> 22.1 us
    pallas_call x1, Pallas kernels: 21.3 us -> 20.7 us  [per_device(): pl.pallas_call(functools.partial(kernel, gy, gz), out_shape=[tile(ROWS, 5...]
where the time goes in v1:
time: 22.2 us; the launch traced here: 22.1 us
  Pallas kernels  22.1 us (100%)
    pallas_call x1, Pallas kernels, per_device(): pl.pallas_call(functools.partial(kernel, gy, gz), out_shape=[tile(ROWS, 5...  20.7 us
    pallas_call x1, Pallas kernels, per_device(): pl.pallas_call(last_kernel, out_shape=jax.ShapeDtypeStruct((8, 5 * ROWS,...  1.32 us

profile of v1, /device:TPU:0, one launch (start us, length us, event | category | flops | bytes accessed | tf_op | source)
XLA Modules:
  0.0 22.1 jit_solution(1120748374914832797)
XLA Ops:
  0.0 20.7 %shard_map.46 = (f32[32,5,8,128]{3,2,1,0:T(8,128)S(1)}, f32[32,4,8,128]{3,2,1,0:T(8,128)S(1)}, f32[20,8,128]{2,1,0:T(8,128)S(1)}) custom-call(f32[8,5,32,128]{3,2,1,0:T(8,128)} %state_h.1, f32[8,32,128]{2,1,0:T(8,128)} %conduct_h.1, f32[8,5,32,128]{3,2,1,0:T(8,128)} %yb_h.1, f32[8,5,32,128]{3,2,1,0:T(8,128)} %zb_h.1), custom_call_target="tpu_custom_call" | custom-call | tf_op jit(solution)/shard_map/pallas_call | solution.py:680
  20.8 1.3 %shard_map.47 = f32[8,160,128]{2,1,0:T(8,128)} custom-call(f32[32,5,8,128]{3,2,1,0:T(8,128)S(1)} %get-tuple-element.8.zval, f32[32,4,8,128]{3,2,1,0:T(8,128)S(1)} %get-tuple-element.9.zspike, f32[20,8,128]{2,1,0:T(8,128)S(1)} %get-tuple-element.10.ends), custom_call_target="tpu_custom_call" | custom-call | tf_op jit(solution)/shard_map/pallas_call | solution.py:701

commit v2 on v1

--- a/solution.py
+++ b/solution.py
@@ -352,8 +352,11 @@
             else:
                 if step > 1:
                     pl.when(jnp.logical_not(owner))(lambda: act(away))
-                local = here.wait if finish else here.start
-                pl.when(owner)(local) if step > 1 else local()
+                if not finish:
+                    pl.when(owner)(here.start) if step > 1 else here.start()
+
+    def scatter_own(out, into, own):
+        pltpu.make_async_copy(out.at[:, 0], into.at[me], own).wait()
 
     def scatter_arrived(out, into, send, recv):
         for k in range(1, gy):
@@ -369,15 +372,17 @@
 
     def own_flux(j, carry):
         k = field[5, j]
-        along = jnp.where(last_lane, zero, flux_tenth * (k + pltpu.roll(k, 127, 1)))
+        upward = jnp.where(last_lane, zero, flux_tenth * (k + pltpu.roll(k, 127, 1)))
+        downward = jnp.where(first_lane, zero, flux_tenth * (k + pltpu.roll(k, 1, 1)))
         across = flux_tenth * (k + field[5, j + 1]) if j < ROWS - 1 else zero
         new = []
         for v in range(5):
             here = field[v, j]
-            z_flow = along * (pltpu.roll(here, 127, 1) - here)
+            before, after = pltpu.roll(here, 1, 1), pltpu.roll(here, 127, 1)
             y_flow = across * (field[v, j + 1] - here) if j < ROWS - 1 else zero
             y_part = y_flow - carry[v] if 0 < j < ROWS - 1 else (y_flow if j == 0 else -carry[v])
-            yval[j, v] = here + (y_part + (z_flow - pltpu.roll(z_flow, 1, 1)))
+            z_part = upward * (after - here) - downward * (here - before)
+            yval[j, v] = here + (y_part + z_part)
             new.append(y_flow)
         return tuple(new)
 
@@ -485,8 +490,8 @@
         return source, target, i
 
     def owner_part():
-        scatter_done(ym_out, ym_in, ym_s, ym_r, own_sem.at[0]) if step == 1 else None
-        scatter_done(yv_out, yv_in, yv_s, yv_r, own_sem.at[1]) if step == 1 else None
+        scatter_own(ym_out, ym_in, own_sem.at[0])
+        scatter_own(yv_out, yv_in, own_sem.at[1])
         owner_solve()
         for k in sorted(range(1, gy), key=lambda k: (6, 7, 4, 5, 2, 3, 1).index(k) if k < 8 else -k):
             source, target, i = ret(k)
@@ -494,13 +499,6 @@
         source, target, i = ret(0)
         pltpu.make_async_copy(source, target, own_sem.at[2]).start()
 
-    if step > 1:
-        scatter_done(ym_out, ym_in, ym_s, ym_r, own_sem.at[0])
-        scatter_done(yv_out, yv_in, yv_s, yv_r, own_sem.at[1])
-        pl.when(owner)(owner_part)
-    else:
-        owner_part()
-
     factor_segment(lambda k, j: zbt[k, pl.ds(j, 8, stride=STEP), :], zcoef, zspike)
     level_0 = end_spikes(zspike)
     level_1, use_1 = merge_matrices(level_0, tuple(up(m, 1) for m in level_0))
@@ -538,6 +536,8 @@
     for b in range(4):
         zm_all[mz, b] = pack_four(level_2[b])
     gather(zm_all, zm_s, zm_r)
+
+    pl.when(owner)(owner_part) if step > 1 else owner_part()
 
     def y_returned():
         for k in range(8):
@@ -639,6 +639,8 @@
             remote(source, target, yr_s.at[k], yr_r.at[place_of_mine], (i, mz)).wait_send()
 
     pl.when(owner)(returns_sent) if step > 1 else returns_sent()
+    scatter_done(ym_out, ym_in, ym_s, ym_r, own_sem.at[0])
+    scatter_done(yv_out, yv_in, yv_s, yv_r, own_sem.at[1])
     gather_sent(zm_all, zm_s, zm_r)
     gather_sent(zv_all, zv_s, zv_r)
 

time: 22.2 us -> 22.1 us (level)
  no operation moved by 1% of the time
where the time goes in v2:
time: 22.1 us; the launch traced here: 21.9 us
  Pallas kernels  21.9 us (99%)
    pallas_call x1, Pallas kernels, per_device(): pl.pallas_call(functools.partial(kernel, gy, gz), out_shape=[tile(ROWS, 5...  20.6 us
    pallas_call x1, Pallas kernels, per_device(): pl.pallas_call(last_kernel, out_shape=jax.ShapeDtypeStruct((8, 5 * ROWS,...  1.32 us

profile of v2, /device:TPU:0, one launch (start us, length us, event | category | flops | bytes accessed | tf_op | source)
XLA Modules:
  0.0 21.9 jit_solution(1295683145653347337)
XLA Ops:
  0.0 20.6 %shard_map.46 = (f32[32,5,8,128]{3,2,1,0:T(8,128)S(1)}, f32[32,4,8,128]{3,2,1,0:T(8,128)S(1)}, f32[20,8,128]{2,1,0:T(8,128)S(1)}) custom-call(f32[8,5,32,128]{3,2,1,0:T(8,128)} %state_h.1, f32[8,32,128]{2,1,0:T(8,128)} %conduct_h.1, f32[8,5,32,128]{3,2,1,0:T(8,128)} %yb_h.1, f32[8,5,32,128]{3,2,1,0:T(8,128)} %zb_h.1), custom_call_target="tpu_custom_call" | custom-call | tf_op jit(solution)/shard_map/pallas_call | solution.py:682
  20.6 1.3 %shard_map.47 = f32[8,160,128]{2,1,0:T(8,128)} custom-call(f32[32,5,8,128]{3,2,1,0:T(8,128)S(1)} %get-tuple-element.8.zval, f32[32,4,8,128]{3,2,1,0:T(8,128)S(1)} %get-tuple-element.9.zspike, f32[20,8,128]{2,1,0:T(8,128)S(1)} %get-tuple-element.10.ends), custom_call_target="tpu_custom_call" | custom-call | tf_op jit(solution)/shard_map/pallas_call | solution.py:703

commit v3 on v2

--- a/solution.py
+++ b/solution.py
@@ -267,9 +267,12 @@
             )
         )
     ]
-    for load in loads:
-        for copy in load:
-            copy.start()
+    def start_loads(*numbers):
+        for k in numbers:
+            for copy in loads[k]:
+                copy.start()
+
+    start_loads(0, 1)
 
     def loaded(k):
         for copy in loads[k]:
@@ -287,6 +290,7 @@
 
     loaded(0)
     loaded(1)
+    start_loads(2, 3)
 
     def pack_row(j, carry):
         a0, a1, b0, b1 = carry
@@ -533,6 +537,31 @@
 
         partners(act)
 
+    def parts_of(device):
+        ends = (device == 0, device == gz - 1)
+        middle = jnp.logical_not(jnp.logical_or(*ends))
+        return zip((*ends, middle), (pl.ds(2, 3), pl.ds(0, 3), pl.ds(0, 5)))
+
+    def values_out(finish):
+        def act(there):
+            for wanted, part in parts_of(mz):
+                mine = zv_all.at[mz, part]
+                away = remote(mine, mine, zv_s.at[there], zv_r.at[mz], (me, there))
+                pl.when(wanted)(away.wait_send if finish else away.start)
+
+        partners(act)
+
+    def values_in():
+        def act(there):
+            for wanted, part in parts_of(there):
+                theirs = zv_all.at[there, part]
+                away = remote(
+                    zv_all.at[mz, part], theirs, zv_s.at[there], zv_r.at[there], (me, there)
+                )
+                pl.when(wanted)(away.wait_recv)
+
+        partners(act)
+
     for b in range(4):
         zm_all[mz, b] = pack_four(level_2[b])
     gather(zm_all, zm_s, zm_r)
@@ -575,9 +604,9 @@
         gh2, gt2, tau2, eta2 = merge_values(use_2, gh1, gt1, up(gh1, 2), up(gt1, 2))
         merged.append((gh2 + gt2, tau1, eta1, tau2, eta2))
     for q in range(4):
-        zv_all[mz, q] = pack_four([merged[v][0][q] for v in range(4)])
-    zv_all[mz, 4] = pack_four([merged[4][0][q] for q in range(4)])
-    gather(zv_all, zv_s, zv_r)
+        zv_all[mz, (0, 1, 3, 4)[q]] = pack_four([merged[v][0][q] for v in range(4)])
+    zv_all[mz, 2] = pack_four([merged[4][0][q] for q in range(4)])
+    values_out(False)
 
     gathered(zm_all, zm_s, zm_r)
 
@@ -592,13 +621,13 @@
         return tuple(tuple(spread(zm_all[i, b], k) for k in range(4)) for b in range(4))
 
     factors = chain_factor(gz, z_matrices)
-    gathered(zv_all, zv_s, zv_r)
+    values_in()
 
     def z_ends(i):
-        return (zv_all[i, 0], zv_all[i, 1]), (zv_all[i, 2], zv_all[i, 3])
+        return (zv_all[i, 0], zv_all[i, 1]), (zv_all[i, 3], zv_all[i, 4])
 
     def z_ends_last(i):
-        tiles = [pltpu.roll(zv_all[i, 4], (8 - q) % 8, 0) if q else zv_all[i, 4] for q in range(4)]
+        tiles = [pltpu.roll(zv_all[i, 2], (8 - q) % 8, 0) if q else zv_all[i, 2] for q in range(4)]
         return (tiles[0], tiles[1]), (tiles[2], tiles[3])
 
     for number, ends in enumerate((z_ends, z_ends_last)):
@@ -642,7 +671,7 @@
     scatter_done(ym_out, ym_in, ym_s, ym_r, own_sem.at[0])
     scatter_done(yv_out, yv_in, yv_s, yv_r, own_sem.at[1])
     gather_sent(zm_all, zm_s, zm_r)
-    gather_sent(zv_all, zv_s, zv_r)
+    values_out(True)
 
 
 def last_kernel(zval, zspike, ends, out, plane, block, sems):

time: 22.1 us -> 21.8 us (0.986)
    pallas_call x1, Pallas kernels: 20.6 us -> 20.3 us  [per_device(): pl.pallas_call(functools.partial(kernel, gy, gz), out_shape=[tile(ROWS, 5...]
where the time goes in v3:
time: 21.8 us; the launch traced here: 21.7 us
  Pallas kernels  21.7 us (100%)
    pallas_call x1, Pallas kernels, per_device(): pl.pallas_call(functools.partial(kernel, gy, gz), out_shape=[tile(ROWS, 5...  20.3 us
    pallas_call x1, Pallas kernels, per_device(): pl.pallas_call(last_kernel, out_shape=jax.ShapeDtypeStruct((8, 5 * ROWS,...  1.32 us

profile of v3, /device:TPU:0, one launch (start us, length us, event | category | flops | bytes accessed | tf_op | source)
XLA Modules:
  0.0 21.7 jit_solution(2880480335638358)
XLA Ops:
  0.0 20.3 %shard_map.46 = (f32[32,5,8,128]{3,2,1,0:T(8,128)S(1)}, f32[32,4,8,128]{3,2,1,0:T(8,128)S(1)}, f32[20,8,128]{2,1,0:T(8,128)S(1)}) custom-call(f32[8,5,32,128]{3,2,1,0:T(8,128)} %state_h.1, f32[8,32,128]{2,1,0:T(8,128)} %conduct_h.1, f32[8,5,32,128]{3,2,1,0:T(8,128)} %yb_h.1, f32[8,5,32,128]{3,2,1,0:T(8,128)} %zb_h.1), custom_call_target="tpu_custom_call" | custom-call | tf_op jit(solution)/shard_map/pallas_call | solution.py:711
  20.3 1.3 %shard_map.47 = f32[8,160,128]{2,1,0:T(8,128)} custom-call(f32[32,5,8,128]{3,2,1,0:T(8,128)S(1)} %get-tuple-element.8.zval, f32[32,4,8,128]{3,2,1,0:T(8,128)S(1)} %get-tuple-element.9.zspike, f32[20,8,128]{2,1,0:T(8,128)S(1)} %get-tuple-element.10.ends), custom_call_target="tpu_custom_call" | custom-call | tf_op jit(solution)/shard_map/pallas_call | solution.py:732
